TPU v7x, 128 devices: a whole 4x4x4 slice. The times are simulated.
128 devices in a mesh: row: 8 (over y, x_lo), col: 16 (over z, x_hi, core).
Axes of the slice: x: 4 (x_hi: 2, x_lo: 2; x = x_hi * 2 + x_lo), y: 4, z: 4, core: 2. Of those that a mesh axis runs over, the one named last changes fastest.
Arguments:
- pair: bfloat16 [256, 256, 128], P('row', 'col'), may hold values from -6 to 6
- cotangent: bfloat16 [256, 256, 128], P('row', 'col'), may hold values from -6 to 6
- token_mask: int32 [256], replicated, may hold values 0 or 1
- out_in_proj: bfloat16 [128, 640], replicated, may hold values from -0.5 to 0.5
- out_out_proj: bfloat16 [128, 128], replicated, may hold values from -0.5 to 0.5
- in_in_proj: bfloat16 [128, 640], replicated, may hold values from -0.5 to 0.5
- in_out_proj: bfloat16 [128, 128], replicated, may hold values from -0.5 to 0.5
Outputs:
- updated_pair: bfloat16 [256, 256, 128], P('row', 'col')
- pair_grad: bfloat16 [256, 256, 128], P('row', 'col')
- out_in_grad: float32 [128, 640], replicated
- out_out_grad: float32 [128, 128], replicated
- in_in_grad: float32 [128, 640], replicated
- in_out_grad: float32 [128, 128], replicated
All inputs are finite; a program needn't handle non-finite values.
Results may differ from a plain program's by a relative error of at most 0.012.
Values may be sent and summed in bfloat16 or wider, within the bound.
A program may use at most 128 MiB of HBM per device.

v0:
```python
import jax
import jax.numpy as jnp
from jax import lax
from jax.sharding import PartitionSpec as P

H = 128
EPSILON = 1e-05


def shortened(array):
    return jax.tree.map(lambda a: a.astype(jnp.bfloat16) if a.dtype == jnp.float32 else a, array)


def from_everyone(array, axis):
    copies = jnp.broadcast_to(array, (lax.axis_size(axis), *array.shape))
    return lax.all_to_all(copies, axis, split_axis=0, concat_axis=0, tiled=True)


def in_order(tiles, dim):
    shape = list(tiles.shape[1:])
    shape[dim] *= tiles.shape[0]
    return jnp.moveaxis(tiles, 0, dim).reshape(shape)


def collect(array, axis, dim):
    tiles = from_everyone(array, axis)
    return in_order(tiles, dim)


def normalize(values):
    centre = jnp.mean(values, axis=-1, keepdims=True)
    shifted = values - centre
    spread = jnp.mean(shifted * shifted, axis=-1, keepdims=True)
    return shifted * lax.rsqrt(spread + EPSILON)


def gating(projected, pair_mask):
    left_value = projected[..., :H]
    left_gate = projected[..., H : 2 * H]
    right_value = projected[..., 2 * H : 3 * H]
    right_gate = projected[..., 3 * H : 4 * H]
    left_full = jax.nn.sigmoid(left_gate) * left_value * pair_mask
    right_full = jax.nn.sigmoid(right_gate) * right_value * pair_mask
    return (left_full, right_full, jax.nn.sigmoid(projected[..., 4 * H :]))


def cols_of(tiles):
    return jax.tree.map(
        lambda part, own: part.astype(own.dtype),
        lax.all_gather(shortened(tiles), "col", axis=1, tiled=True),
        tiles,
    )


def rows_of(tiles):
    return jax.tree.map(
        lambda part, own: part.astype(own.dtype),
        jax.tree.map(lambda part: collect(part, "row", 0), shortened(tiles)),
        tiles,
    )


def to_row_blocks(panel):
    return lax.all_to_all(panel, "col", split_axis=0, concat_axis=1, tiled=True)


def to_col_blocks(panel):
    return lax.all_to_all(panel, "row", split_axis=1, concat_axis=0, tiled=True)


def outgoing_sum(left_tile, right_tile):
    row_panels = rows_of((left_tile, right_tile))
    left_panel = cols_of(left_tile)
    right_rows = to_row_blocks(row_panels[1])
    total = jnp.einsum("ikh,jkh->ijh", left_panel, right_rows, preferred_element_type=jnp.float32)
    return (total, row_panels)


def incoming_sum(left_tile, right_tile):
    col_panels = cols_of((left_tile, right_tile))
    right_all = rows_of(right_tile)
    left_cols = to_col_blocks(col_panels[0])
    total = jnp.einsum("kih,kjh->ijh", left_cols, right_all, preferred_element_type=jnp.float32)
    return (total, col_panels)


def outgoing_grads(tri_grad, row_panels):
    grad_cols = cols_of(tri_grad)
    grad_rows = to_col_blocks(grad_cols)
    left_grad = jnp.einsum(
        "ijh,jkh->ikh", grad_cols, row_panels[1], preferred_element_type=jnp.float32
    )
    right_grad = jnp.einsum(
        "ijh,ikh->jkh", grad_rows, row_panels[0], preferred_element_type=jnp.float32
    )
    return (left_grad, right_grad)


def incoming_grads(tri_grad, col_panels):
    grad_rows = rows_of(tri_grad)
    grad_cols = to_row_blocks(grad_rows)
    left_grad = jnp.einsum(
        "ijh,kjh->kih", grad_cols, col_panels[1], preferred_element_type=jnp.float32
    )
    right_grad = jnp.einsum(
        "kih,ijh->kjh", col_panels[0], grad_rows, preferred_element_type=jnp.float32
    )
    return (left_grad, right_grad)


def forward(pair_in, pair_mask, w_in, w_out, outgoing):
    pair_wide = pair_in.astype(jnp.float32)
    normed = normalize(pair_wide).astype(jnp.bfloat16)
    projected = jnp.dot(normed, w_in, preferred_element_type=jnp.float32)
    left_full, right_full, gate = gating(projected, pair_mask)
    left_tile = left_full.astype(jnp.bfloat16)
    right_tile = right_full.astype(jnp.bfloat16)
    if outgoing:
        triangle_sum, panels = outgoing_sum(left_tile, right_tile)
    else:
        triangle_sum, panels = incoming_sum(left_tile, right_tile)
    tri_normed = normalize(triangle_sum).astype(jnp.bfloat16)
    lifted = jnp.dot(tri_normed, w_out, preferred_element_type=jnp.float32)
    result = (pair_wide + gate * lifted).astype(jnp.bfloat16)
    saved = (pair_wide, normed, projected, gate, triangle_sum, tri_normed, lifted, panels)
    return (result, saved)


def backward(cotan, saved, pair_mask, w_in, w_out, outgoing):
    pair_wide, normed, projected, gate, triangle_sum, tri_normed, lifted, panels = saved
    cot_wide = cotan.astype(jnp.float32)
    lift_grad = gate * cot_wide
    gate_grad = lifted * cot_wide
    out_grad = jnp.einsum(
        "ijh,ijc->hc", tri_normed.astype(jnp.float32), lift_grad, precision=lax.Precision.HIGHEST
    )
    normed_tri_grad = jnp.dot(
        lift_grad, w_out.astype(jnp.float32).T, precision=lax.Precision.HIGHEST
    )
    tri_grad = jax.vjp(normalize, triangle_sum)[1](normed_tri_grad)[0].astype(jnp.bfloat16)
    if outgoing:
        left_grad, right_grad = outgoing_grads(tri_grad, panels)
    else:
        left_grad, right_grad = incoming_grads(tri_grad, panels)
    gate_vjp = jax.vjp(lambda values: gating(values, pair_mask), projected)[1]
    proj_grad = gate_vjp((left_grad, right_grad, gate_grad))[0]
    in_grad = jnp.einsum(
        "ijc,ijq->cq", normed.astype(jnp.float32), proj_grad, precision=lax.Precision.HIGHEST
    )
    normed_grad = jnp.dot(proj_grad, w_in.astype(jnp.float32).T, precision=lax.Precision.HIGHEST)
    pair_grad = (cot_wide + jax.vjp(normalize, pair_wide)[1](normed_grad)[0]).astype(jnp.bfloat16)
    return (pair_grad, in_grad, out_grad)


def local(pair, cotangent, token_mask, out_in_proj, out_out_proj, in_in_proj, in_out_proj):
    row_tile = pair.shape[0]
    col_tile = pair.shape[1]
    row_flags = lax.dynamic_slice_in_dim(
        token_mask, lax.axis_index("row") * row_tile, row_tile, 0
    ).astype(jnp.float32)
    col_flags = lax.dynamic_slice_in_dim(
        token_mask, lax.axis_index("col") * col_tile, col_tile, 0
    ).astype(jnp.float32)
    pair_mask = (row_flags[:, None] * col_flags[None, :])[:, :, None]
    middle, saved_out = forward(pair, pair_mask, out_in_proj, out_out_proj, True)
    updated, saved_in = forward(middle, pair_mask, in_in_proj, in_out_proj, False)
    middle_grad, in_in_part, in_out_part = backward(
        cotangent, saved_in, pair_mask, in_in_proj, in_out_proj, False
    )
    pair_grad, out_in_part, out_out_part = backward(
        middle_grad, saved_out, pair_mask, out_in_proj, out_out_proj, True
    )
    totals = lax.psum((out_in_part, out_out_part, in_in_part, in_out_part), ("row", "col"))
    tokens_all = row_tile * lax.axis_size("row")
    return (
        updated,
        pair_grad,
        totals[0] / tokens_all,
        totals[1] / tokens_all,
        totals[2] / tokens_all,
        totals[3] / tokens_all,
    )


def solution(mesh):
    return jax.shard_map(
        local,
        mesh=mesh,
        in_specs=(P("row", "col", None), P("row", "col", None), P(), P(), P(), P(), P()),
        out_specs=(P("row", "col", None), P("row", "col", None), P(), P(), P(), P()),
        check_vma=False,
    )
```

profile of v0, /device:TPU:1, one launch (start us, length us, event | category | flops | bytes accessed | tf_op | source)
XLA Modules:
  0.0 564.3 jit_solution(1086619950908574980)
XLA Ops:
  14.3 22.1 %all_to_all.92 = bf16[8,32,16,128]{3,2,1,0:T(8,128)(2,1)S(1)} all-to-all(bf16[8,32,16,128]{3,2,1,0:T(8,128)(2,1)S(1)} %broadcast_in_dim.24), channel_id=1, replica_groups=mesh['row'=8,'col'=16] {'row'}, dimensions={0} | all-to-all | bytes 2097152 | tf_op jit(solution)/shard_map/all_to_all | solution.py:16
  36.4 31.5 %all_to_all.93 = bf16[256,16,128]{2,1,0:T(8,128)(2,1)S(1)} all-to-all(bf16[256,16,128]{2,1,0:T(8,128)(2,1)S(1)} %bitcast.135), channel_id=1, replica_groups=mesh['row'=8,'col'=16] {'col'}, dimensions={0} | all-to-all | bytes 2097152 | tf_op jit(solution)/shard_map/all_to_all | solution.py:64
  69.1 2.7 copy.220
  72.3 15.3 %copy.221 = bf16[32,256,128]{0,1,2:T(8,128)(2,1)} copy(bf16[32,256,128]{2,1,0:T(8,128)(2,1)} %all-gather.5.cloned.1.call-done) | data formatting | bytes 4194304 | tf_op jit(solution)/shard_map/all_gather | solution.py:50
  87.6 6.0 %bitcast_reduce_fusion.1 = (f32[32,16]{0,1:T(8,128)S(1)}, f32[128,16,32]{2,1,0:T(8,128)}) fusion(bf16[16,256,128]{1,0,2:T(8,128)(2,1)} %copy.220, bf16[32,256,128]{0,1,2:T(8,128)(2,1)} %copy.221), kind=kOutput, calls=%fused_computation.7 | convolution fusion | flops 33619456 | bytes 3409920 | tf_op jit(solution)/shard_map/ikh,jkh->ijh/dot_general | solution.py:75
  101.4 4.2 all-to-all-start.2
  105.7 40.1 %all-gather.7.cloned.1.call-done = bf16[32,256,128]{2,1,0:T(8,128)(2,1)} async-done(((bf16[32,16,128]{2,1,0:T(8,128)(2,1)}), bf16[32,256,128]{2,1,0:T(8,128)(2,1)}) %all-gather.7.cloned.1.call-update) | async-done | bytes 2097168 | tf_op jit(solution)/shard_map/all_gather | solution.py:50
  145.8 4.3 copy.231
  150.1 4.4 all-to-all-start.3
  155.2 3.0 copy.234
  158.2 24.5 %all-to-all-done.3 = bf16[32,256,128]{2,0,1:T(8,128)(2,1)} async-done(((bf16[32,256,128]{2,0,1:T(8,128)(2,1)}), bf16[32,256,128]{2,0,1:T(8,128)(2,1)}, u32[]{:S(2)}, u32[]{:S(2)}) %all-to-all-start.3) | async-done | bytes 2097184 | tf_op jit(solution)/shard_map/all_to_all | solution.py:68
  182.6 3.7 copy.233
  186.4 4.9 copy.235
  191.3 3.6 bitcast_reduce_fusion
  201.9 17.9 %all_to_all.94 = bf16[8,32,16,128]{3,2,1,0:T(8,128)(2,1)} all-to-all(bf16[8,32,16,128]{3,2,1,0:T(8,128)(2,1)S(1)} %broadcast_in_dim.28), channel_id=1, replica_groups=mesh['row'=8,'col'=16] {'row'}, dimensions={0} | all-to-all | bytes 2097152 | tf_op jit(solution)/shard_map/all_to_all | solution.py:16
  219.8 6.1 %all-to-all-start.5 = ((bf16[256,16,128]{2,1,0:T(8,128)(2,1)}), bf16[256,16,128]{2,1,0:T(8,128)(2,1)}, u32[]{:S(2)}, u32[]{:S(2)}) async-start(bf16[256,16,128]{2,1,0:T(8,128)(2,1)} %bitcast.137), calls=%async_computation.5 | async-start | bytes 2097152 | tf_op jit(solution)/shard_map/all_to_all | solution.py:64
  225.9 15.2 %copy.246 = bf16[32,256,128]{0,1,2:T(8,128)(2,1)} copy(bf16[32,256,128]{2,1,0:T(8,128)(2,1)} %all-gather.7.cloned.1.call-done) | data formatting | bytes 4194304 | tf_op jit(solution)/shard_map/all_gather | solution.py:50
  241.2 15.3 %copy.249 = bf16[32,256,128]{0,1,2:T(8,128)(2,1)} copy(bf16[32,256,128]{2,1,0:T(8,128)(2,1)} %all-gather.9.cloned.1.call-done) | data formatting | bytes 4194304 | tf_op jit(solution)/shard_map/all_gather | solution.py:50
  256.5 3.0 copy.245
  259.4 5.9 %fusion.83 = f32[128,16,32]{2,1,0:T(8,128)} fusion(bf16[256,16,128]{0,1,2:T(8,128)(2,1)} %copy.245, bf16[32,256,128]{0,1,2:T(8,128)(2,1)} %copy.246), kind=kOutput, calls=%fused_computation.151 | convolution fusion | flops 33554432 | bytes 3407872 | tf_op jit(solution)/shard_map/kih,ijh->kjh/dot_general | solution.py:105
  270.2 2.7 copy.250
  272.9 5.9 %fusion.86 = f32[128,32,16]{1,2,0:T(8,128)} fusion(bf16[16,256,128]{1,0,2:T(8,128)(2,1)} %copy.250, bf16[32,256,128]{0,1,2:T(8,128)(2,1)} %copy.249), kind=kOutput, calls=%fused_computation.154 | convolution fusion | flops 33554432 | bytes 3407872 | tf_op jit(solution)/shard_map/ijh,kjh->kih/dot_general | solution.py:102
  305.2 4.2 all-to-all-start.6
  309.5 42.8 %all-gather.11.cloned.1.call-done = bf16[32,256,128]{2,1,0:T(8,128)(2,1)} async-done(((bf16[32,16,128]{2,1,0:T(8,128)(2,1)}), bf16[32,256,128]{2,1,0:T(8,128)(2,1)}) %all-gather.11.cloned.1.call-update) | async-done | bytes 2097168 | tf_op jit(solution)/shard_map/all_gather | solution.py:50
  352.3 4.3 copy.260
  356.6 4.3 all-to-all-start.7
  363.3 3.1 copy.263
  371.3 15.3 %copy.267 = bf16[32,256,128]{0,1,2:T(8,128)(2,1)} copy(bf16[32,256,128]{2,1,0:T(8,128)(2,1)} %all-gather.11.cloned.1.call-done) | data formatting | bytes 4194304 | tf_op jit(solution)/shard_map/all_gather | solution.py:50
  386.6 4.9 fusion.85
  392.0 3.7 copy.262
  395.7 4.9 copy.264
  408.7 145.6 %all-reduce.13.cloned.1.call-done = (f32[128,640]{1,0:T(8,128)}, f32[128,128]{1,0:T(8,128)}, f32[128,640]{1,0:T(8,128)}, f32[128,128]{1,0:T(8,128)}) async-done(((f32[128,640]{1,0:T(8,128)}, f32[128,128]{1,0:T(8,128)}, f32[128,640]{1,0:T(8,128)}, f32[128,128]{1,0:T(8,128)}), (f32[128,640]{1,0:T(8,128)}, f32[128,128]{1,0:T(8,128)}, f32[128,640]{1,0:T(8,128)}, ...) | async-done | bytes 786448 | tf_op jit(solution)/shard_map/psum | solution.py:173
  (171 shorter events, 74.7 us)
Async XLA Ops:
  7.2 90.8 %copy-start = (bf16[128,640]{1,0:T(8,128)(2,1)S(1)}, bf16[128,640]{1,0:T(8,128)(2,1)}, u32[]{:S(2)}) copy-start(bf16[128,640]{1,0:T(8,128)(2,1)} %param.12) | copy-start | bytes 491524
  7.2 65.1 %all-gather.5.cloned.1.call-start = ((), (), s32[]{:S(2)}) async-start(), calls=%async_computation.8 | async-start | bytes 2228224 | tf_op jit(solution)/shard_map/all_gather | solution.py:50
  14.1 131.7 %all-gather.7.cloned.1.call-start = ((), (), s32[]{:S(2)}) async-start(), calls=%async_computation.9 | async-start | bytes 2228224 | tf_op jit(solution)/shard_map/all_gather | solution.py:50
  93.6 2.2 copy-start.2
  93.6 2.2 copy-start.21
  95.7 1.6 copy-start.17
  101.4 48.6 %all-to-all-start.2 = ((bf16[8,32,16,128]{3,2,1,0:T(8,128)(2,1)}), bf16[8,32,16,128]{3,2,1,0:T(8,128)(2,1)}, u32[]{:S(2)}, u32[]{:S(2)}) async-start(bf16[8,32,16,128]{3,2,1,0:T(8,128)(2,1)} %broadcast_in_dim.25), calls=%async_computation.2 | async-start | bytes 2097152 | tf_op jit(solution)/shard_map/all_to_all | solution.py:16
  150.1 32.6 %all-to-all-start.3 = ((bf16[32,256,128]{2,0,1:T(8,128)(2,1)}), bf16[32,256,128]{2,0,1:T(8,128)(2,1)}, u32[]{:S(2)}, u32[]{:S(2)}) async-start(bf16[32,256,128]{2,0,1:T(8,128)(2,1)} %copy.231), calls=%async_computation.3 | async-start | bytes 4194304 | tf_op jit(solution)/shard_map/all_to_all | solution.py:68
  154.4 86.7 %all-gather.9.cloned.1.call-start = ((), (), s32[]{:S(2)}) async-start(), calls=%async_computation.10 | async-start | bytes 2228224 | tf_op jit(solution)/shard_map/all_gather | solution.py:50
  194.8 1.8 copy-start.20
  196.6 84.6 %copy-start.10 = (f32[32,16]{1,0:T(8,128)}, f32[32,16]{1,0:T(8,128)S(1)}, u32[]{:S(2)}) copy-start(f32[32,16]{1,0:T(8,128)S(1)} %copy.238) | copy-start | bytes 6148
  198.9 82.3 %copy-start.12 = (f32[32,16]{1,0:T(8,128)}, f32[32,16]{1,0:T(8,128)S(1)}, u32[]{:S(2)}) copy-start(f32[32,16]{1,0:T(8,128)S(1)} %copy.240) | copy-start | bytes 6148
  219.8 47.9 %all-to-all-start.5 = ((bf16[256,16,128]{2,1,0:T(8,128)(2,1)}), bf16[256,16,128]{2,1,0:T(8,128)(2,1)}, u32[]{:S(2)}, u32[]{:S(2)}) async-start(bf16[256,16,128]{2,1,0:T(8,128)(2,1)} %bitcast.137), calls=%async_computation.5 | async-start | bytes 2097152 | tf_op jit(solution)/shard_map/all_to_all | solution.py:64
  225.9 126.4 %all-gather.11.cloned.1.call-start = ((), (), s32[]{:S(2)}) async-start(), calls=%async_computation.11 | async-start | bytes 2228224 | tf_op jit(solution)/shard_map/all_gather | solution.py:50
  283.7 1.5 copy-start.22
  283.7 1.5 copy-start.24
  283.7 1.5 copy-start.26
  283.8 1.5 copy-start.28
  283.8 1.5 copy-start.30
  283.8 1.5 copy-start.19
  289.6 14.5 %copy-start.3 = (bf16[32,16,128]{2,1,0:T(8,128)(2,1)S(1)}, bf16[32,16,128]{2,1,0:T(8,128)(2,1)}, u32[]{:S(2)}) copy-start(bf16[32,16,128]{2,1,0:T(8,128)(2,1)} %get-tuple-element.32) | copy-start | bytes 393220
  305.2 51.4 %all-to-all-start.6 = ((bf16[8,32,16,128]{3,2,1,0:T(8,128)(2,1)}), bf16[8,32,16,128]{3,2,1,0:T(8,128)(2,1)}, u32[]{:S(2)}, u32[]{:S(2)}) async-start(bf16[8,32,16,128]{3,2,1,0:T(8,128)(2,1)} %broadcast_in_dim.62), calls=%async_computation.6 | async-start | bytes 2097152 | tf_op jit(solution)/shard_map/all_to_all | solution.py:16
  356.6 35.4 %all-to-all-start.7 = ((bf16[32,256,128]{2,0,1:T(8,128)(2,1)}), bf16[32,256,128]{2,0,1:T(8,128)(2,1)}, u32[]{:S(2)}, u32[]{:S(2)}) async-start(bf16[32,256,128]{2,0,1:T(8,128)(2,1)} %copy.260), calls=%async_computation.7 | async-start | bytes 4194304 | tf_op jit(solution)/shard_map/all_to_all | solution.py:68
  360.9 193.3 %all-reduce.13.cloned.1.call-start = ((), (), s32[]{:S(2)}) async-start(), calls=%async_computation.12 | async-start | bytes 1572864 | tf_op jit(solution)/shard_map/psum | solution.py:173
  363.3 3.1 copy-start.11
  363.3 3.1 copy-start.13
  363.3 3.1 copy-start.14
  366.4 2.1 copy-start.6
  368.5 1.2 copy-start.29
  368.5 1.2 copy-start.31
  404.6 1.5 copy-start.8
  404.6 1.5 copy-start.9
  (10 other events, 9.3 us)
Sparse Core Ops, SparseCore 0:
  14.2 58.0 all-gather.4
  100.5 45.2 all-gather.6
  157.6 47.5 all-gather.8
  304.2 48.0 all-gather.10
  407.7 146.5 all-reduce.12
where the time goes:
time: 566 us; the launch traced here: 564 us
  waiting for transfers between devices  254 us (45%)
  local copies, waits for them, and re-layouts  130 us (23%)
  blocking collectives  71.5 us (13%)
  matrix products  47.2 us (8%)
  starting transfers between devices  23.8 us (4%)
  other arithmetic  23.6 us (4%)
  between operations  14.2 us (3%)
    psum x1, waiting for transfers between devices, local(): lax.psum((out_in_part, out_out_part, in_in_part, in_out_part), ('row', 'c...  146 us
    all_gather x4, waiting for transfers between devices, cols_of(): lax.all_gather(shortened(tiles), 'col', axis=1, tiled=True)  83.4 us
    all_gather x6, local copies, waits for them, and re-layouts, cols_of(): lax.all_gather(shortened(tiles), 'col', axis=1, tiled=True)  69.7 us
    all_to_all x2, blocking collectives, from_everyone(): return lax.all_to_all(copies, axis, split_axis=0, concat_axis=0, tiled=True)  40 us
    all_to_all x1, blocking collectives, to_row_blocks(): return lax.all_to_all(panel, 'col', split_axis=0, concat_axis=1, tiled=True)  31.5 us
    all_to_all x2, waiting for transfers between devices, to_col_blocks(): return lax.all_to_all(panel, 'row', split_axis=1, concat_axis=0, tiled=True)  24.5 us
    all_to_all x4, local copies, waits for them, and re-layouts, to_col_blocks(): return lax.all_to_all(panel, 'row', split_axis=1, concat_axis=0, tiled=True)  17.2 us
  transfers between devices with their start and end apart: 10, of which 5 were waited for; matrix products, arithmetic and copies ran while one was open for 20% of the time, Pallas kernels for 0%

commit v1 on v0

--- a/solution.py
+++ b/solution.py
@@ -170,7 +170,7 @@
     pair_grad, out_in_part, out_out_part = backward(
         middle_grad, saved_out, pair_mask, out_in_proj, out_out_proj, True
     )
-    totals = lax.psum((out_in_part, out_out_part, in_in_part, in_out_part), ("row", "col"))
+    totals = lax.psum(lax.psum((out_in_part, out_out_part, in_in_part, in_out_part), "col"), "row")
     tokens_all = row_tile * lax.axis_size("row")
     return (
         updated,

time: 566 us -> 653 us (1.15); the launches traced: 564 us -> 641 us
  waiting for transfers between devices: 254 us -> 323 us
  starting transfers between devices: 23.8 us -> 31.7 us
    psum x1 -> x2, waiting for transfers between devices: 146 us -> 214 us  [the longest x1 138 us: local(): lax.psum((out_in_part, out_out_part, in_in_part, in_out_part), 'col')]
    psum x1 -> x2, starting transfers between devices: 0.26 us -> 8.01 us  [the longest x1 7.97 us: local(): lax.psum((out_in_part, out_out_part, in_in_part, in_out_part), 'col')]
  transfers between devices with their start and end apart: 10 -> 11, of which waited for: 5 -> 6; matrix products, arithmetic and copies ran while one was open for 20% -> 17% of each run, Pallas kernels for 0% -> 0%
where the time goes in v1:
time: 653 us; the launch traced here: 641 us
  waiting for transfers between devices  323 us (49%)
  local copies, waits for them, and re-layouts  130 us (20%)
  blocking collectives  71.5 us (11%)
  matrix products  47.2 us (7%)
  starting transfers between devices  31.7 us (5%)
  other arithmetic  23.6 us (4%)
  between operations  14.5 us (2%)
    psum x1, waiting for transfers between devices, local(): lax.psum((out_in_part, out_out_part, in_in_part, in_out_part), 'col')  138 us
    all_gather x4, waiting for transfers between devices, cols_of(): lax.all_gather(shortened(tiles), 'col', axis=1, tiled=True)  83.4 us
    psum x1, waiting for transfers between devices, local(): lax.psum(lax.psum((out_in_part, out_out_part, in_in_part, in_out_part), '...  76 us
    all_gather x6, local copies, waits for them, and re-layouts, cols_of(): lax.all_gather(shortened(tiles), 'col', axis=1, tiled=True)  69.7 us
    all_to_all x2, blocking collectives, from_everyone(): return lax.all_to_all(copies, axis, split_axis=0, concat_axis=0, tiled=True)  40 us
    all_to_all x1, blocking collectives, to_row_blocks(): return lax.all_to_all(panel, 'col', split_axis=0, concat_axis=1, tiled=True)  31.5 us
    all_to_all x2, waiting for transfers between devices, to_col_blocks(): return lax.all_to_all(panel, 'row', split_axis=1, concat_axis=0, tiled=True)  24.5 us
    all_to_all x4, local copies, waits for them, and re-layouts, to_col_blocks(): return lax.all_to_all(panel, 'row', split_axis=1, concat_axis=0, tiled=True)  17.2 us
  transfers between devices with their start and end apart: 11, of which 6 were waited for; matrix products, arithmetic and copies ran while one was open for 17% of the time, Pallas kernels for 0%

profile of v1, /device:TPU:1, one launch (start us, length us, event | category | flops | bytes accessed | tf_op | source)
XLA Modules:
  0.0 641.1 jit_solution(13294625271521838424)
XLA Ops:
  14.3 22.1 %all_to_all.92 = bf16[8,32,16,128]{3,2,1,0:T(8,128)(2,1)S(1)} all-to-all(bf16[8,32,16,128]{3,2,1,0:T(8,128)(2,1)S(1)} %broadcast_in_dim.24), channel_id=1, replica_groups=mesh['row'=8,'col'=16] {'row'}, dimensions={0} | all-to-all | bytes 2097152 | tf_op jit(solution)/shard_map/all_to_all | solution.py:16
  36.4 31.5 %all_to_all.93 = bf16[256,16,128]{2,1,0:T(8,128)(2,1)S(1)} all-to-all(bf16[256,16,128]{2,1,0:T(8,128)(2,1)S(1)} %bitcast.135), channel_id=1, replica_groups=mesh['row'=8,'col'=16] {'col'}, dimensions={0} | all-to-all | bytes 2097152 | tf_op jit(solution)/shard_map/all_to_all | solution.py:64
  72.3 15.3 %copy.221 = bf16[32,256,128]{0,1,2:T(8,128)(2,1)} copy(bf16[32,256,128]{2,1,0:T(8,128)(2,1)} %all-gather.5.cloned.1.call-done) | data formatting | bytes 4194304 | tf_op jit(solution)/shard_map/all_gather | solution.py:50
  87.6 6.0 bitcast_reduce_fusion.1
  101.5 4.2 all-to-all-start.2
  105.7 40.1 %all-gather.7.cloned.1.call-done = bf16[32,256,128]{2,1,0:T(8,128)(2,1)} async-done(((bf16[32,16,128]{2,1,0:T(8,128)(2,1)}), bf16[32,256,128]{2,1,0:T(8,128)(2,1)}) %all-gather.7.cloned.1.call-update) | async-done | bytes 2097168 | tf_op jit(solution)/shard_map/all_gather | solution.py:50
  145.8 4.3 copy.231
  150.1 4.3 all-to-all-start.3
  155.2 3.0 copy.234
  158.2 24.5 %all-to-all-done.3 = bf16[32,256,128]{2,0,1:T(8,128)(2,1)} async-done(((bf16[32,256,128]{2,0,1:T(8,128)(2,1)}), bf16[32,256,128]{2,0,1:T(8,128)(2,1)}, u32[]{:S(2)}, u32[]{:S(2)}) %all-to-all-start.3) | async-done | bytes 2097184 | tf_op jit(solution)/shard_map/all_to_all | solution.py:68
  182.7 3.8 copy.233
  186.4 4.9 copy.235
  191.3 3.6 bitcast_reduce_fusion
  202.0 17.9 %all_to_all.94 = bf16[8,32,16,128]{3,2,1,0:T(8,128)(2,1)} all-to-all(bf16[8,32,16,128]{3,2,1,0:T(8,128)(2,1)S(1)} %broadcast_in_dim.28), channel_id=1, replica_groups=mesh['row'=8,'col'=16] {'row'}, dimensions={0} | all-to-all | bytes 2097152 | tf_op jit(solution)/shard_map/all_to_all | solution.py:16
  219.9 6.1 all-to-all-start.5
  226.0 15.3 %copy.246 = bf16[32,256,128]{0,1,2:T(8,128)(2,1)} copy(bf16[32,256,128]{2,1,0:T(8,128)(2,1)} %all-gather.7.cloned.1.call-done) | data formatting | bytes 4194304 | tf_op jit(solution)/shard_map/all_gather | solution.py:50
  241.3 15.3 %copy.249 = bf16[32,256,128]{0,1,2:T(8,128)(2,1)} copy(bf16[32,256,128]{2,1,0:T(8,128)(2,1)} %all-gather.9.cloned.1.call-done) | data formatting | bytes 4194304 | tf_op jit(solution)/shard_map/all_gather | solution.py:50
  256.6 3.0 copy.245
  259.5 5.9 fusion.83
  273.0 5.9 fusion.86
  305.3 4.2 all-to-all-start.6
  309.6 42.8 %all-gather.11.cloned.1.call-done = bf16[32,256,128]{2,1,0:T(8,128)(2,1)} async-done(((bf16[32,16,128]{2,1,0:T(8,128)(2,1)}), bf16[32,256,128]{2,1,0:T(8,128)(2,1)}) %all-gather.11.cloned.1.call-update) | async-done | bytes 2097168 | tf_op jit(solution)/shard_map/all_gather | solution.py:50
  352.4 4.3 copy.260
  356.7 4.4 all-to-all-start.7
  361.0 8.0 %all-reduce.15.cloned.1.call-start = ((), (), s32[]{:S(2)}) async-start(), calls=%async_computation.12 | async-start | bytes 1572864 | tf_op jit(solution)/shard_map/psum | solution.py:173
  371.1 3.1 copy.263
  379.0 15.3 %copy.267 = bf16[32,256,128]{0,1,2:T(8,128)(2,1)} copy(bf16[32,256,128]{2,1,0:T(8,128)(2,1)} %all-gather.11.cloned.1.call-done) | data formatting | bytes 4194304 | tf_op jit(solution)/shard_map/all_gather | solution.py:50
  394.3 4.9 fusion.85
  399.8 3.7 copy.262
  403.5 4.9 copy.264
  414.9 138.3 %all-reduce.15.cloned.1.call-done = (f32[128,640]{1,0:T(8,128)}, f32[128,128]{1,0:T(8,128)}, f32[128,640]{1,0:T(8,128)}, f32[128,128]{1,0:T(8,128)}) async-done(((f32[128,640]{1,0:T(8,128)}, f32[128,128]{1,0:T(8,128)}, f32[128,640]{1,0:T(8,128)}, f32[128,128]{1,0:T(8,128)}), (f32[128,640]{1,0:T(8,128)}, f32[128,128]{1,0:T(8,128)}, f32[128,640]{1,0:T(8,128)}, ...) | async-done | bytes 786448 | tf_op jit(solution)/shard_map/psum | solution.py:173
  554.8 76.0 %all-reduce.17.cloned.1.call-done = (f32[128,640]{1,0:T(8,128)}, f32[128,128]{1,0:T(8,128)}, f32[128,640]{1,0:T(8,128)}, f32[128,128]{1,0:T(8,128)}) async-done(((f32[128,640]{1,0:T(8,128)}, f32[128,128]{1,0:T(8,128)}, f32[128,640]{1,0:T(8,128)}, f32[128,128]{1,0:T(8,128)}), (f32[128,640]{1,0:T(8,128)}, f32[128,128]{1,0:T(8,128)}, f32[128,640]{1,0:T(8,128)}, ...) | async-done | bytes 786448 | tf_op jit(solution)/shard_map/psum | solution.py:173
  (174 shorter events, 79.9 us)
Async XLA Ops:
  7.2 90.9 %copy-start = (bf16[128,640]{1,0:T(8,128)(2,1)S(1)}, bf16[128,640]{1,0:T(8,128)(2,1)}, u32[]{:S(2)}) copy-start(bf16[128,640]{1,0:T(8,128)(2,1)} %param.12) | copy-start | bytes 491524
  7.2 65.1 %all-gather.5.cloned.1.call-start = ((), (), s32[]{:S(2)}) async-start(), calls=%async_computation.8 | async-start | bytes 2228224 | tf_op jit(solution)/shard_map/all_gather | solution.py:50
  14.1 131.7 %all-gather.7.cloned.1.call-start = ((), (), s32[]{:S(2)}) async-start(), calls=%async_computation.9 | async-start | bytes 2228224 | tf_op jit(solution)/shard_map/all_gather | solution.py:50
  93.6 2.2 copy-start.2
  93.6 2.2 copy-start.21
  95.7 1.6 copy-start.17
  101.5 48.6 %all-to-all-start.2 = ((bf16[8,32,16,128]{3,2,1,0:T(8,128)(2,1)}), bf16[8,32,16,128]{3,2,1,0:T(8,128)(2,1)}, u32[]{:S(2)}, u32[]{:S(2)}) async-start(bf16[8,32,16,128]{3,2,1,0:T(8,128)(2,1)} %broadcast_in_dim.25), calls=%async_computation.2 | async-start | bytes 2097152 | tf_op jit(solution)/shard_map/all_to_all | solution.py:16
  150.1 32.6 %all-to-all-start.3 = ((bf16[32,256,128]{2,0,1:T(8,128)(2,1)}), bf16[32,256,128]{2,0,1:T(8,128)(2,1)}, u32[]{:S(2)}, u32[]{:S(2)}) async-start(bf16[32,256,128]{2,0,1:T(8,128)(2,1)} %copy.231), calls=%async_computation.3 | async-start | bytes 4194304 | tf_op jit(solution)/shard_map/all_to_all | solution.py:68
  154.5 86.8 %all-gather.9.cloned.1.call-start = ((), (), s32[]{:S(2)}) async-start(), calls=%async_computation.10 | async-start | bytes 2228224 | tf_op jit(solution)/shard_map/all_gather | solution.py:50
  194.9 1.8 copy-start.20
  196.7 84.6 %copy-start.10 = (f32[32,16]{1,0:T(8,128)}, f32[32,16]{1,0:T(8,128)S(1)}, u32[]{:S(2)}) copy-start(f32[32,16]{1,0:T(8,128)S(1)} %copy.238) | copy-start | bytes 6148
  199.0 82.3 %copy-start.12 = (f32[32,16]{1,0:T(8,128)}, f32[32,16]{1,0:T(8,128)S(1)}, u32[]{:S(2)}) copy-start(f32[32,16]{1,0:T(8,128)S(1)} %copy.240) | copy-start | bytes 6148
  219.9 48.0 %all-to-all-start.5 = ((bf16[256,16,128]{2,1,0:T(8,128)(2,1)}), bf16[256,16,128]{2,1,0:T(8,128)(2,1)}, u32[]{:S(2)}, u32[]{:S(2)}) async-start(bf16[256,16,128]{2,1,0:T(8,128)(2,1)} %bitcast.137), calls=%async_computation.5 | async-start | bytes 2097152 | tf_op jit(solution)/shard_map/all_to_all | solution.py:64
  225.9 126.5 %all-gather.11.cloned.1.call-start = ((), (), s32[]{:S(2)}) async-start(), calls=%async_computation.11 | async-start | bytes 2228224 | tf_op jit(solution)/shard_map/all_gather | solution.py:50
  283.8 1.5 copy-start.22
  283.8 1.5 copy-start.24
  283.8 1.5 copy-start.26
  283.8 1.5 copy-start.28
  283.8 1.5 copy-start.30
  283.9 1.5 copy-start.19
  289.7 14.5 %copy-start.3 = (bf16[32,16,128]{2,1,0:T(8,128)(2,1)S(1)}, bf16[32,16,128]{2,1,0:T(8,128)(2,1)}, u32[]{:S(2)}) copy-start(bf16[32,16,128]{2,1,0:T(8,128)(2,1)} %get-tuple-element.36) | copy-start | bytes 393220
  305.3 51.3 %all-to-all-start.6 = ((bf16[8,32,16,128]{3,2,1,0:T(8,128)(2,1)}), bf16[8,32,16,128]{3,2,1,0:T(8,128)(2,1)}, u32[]{:S(2)}, u32[]{:S(2)}) async-start(bf16[8,32,16,128]{3,2,1,0:T(8,128)(2,1)} %broadcast_in_dim.62), calls=%async_computation.6 | async-start | bytes 2097152 | tf_op jit(solution)/shard_map/all_to_all | solution.py:16
  356.7 43.1 %all-to-all-start.7 = ((bf16[32,256,128]{2,0,1:T(8,128)(2,1)}), bf16[32,256,128]{2,0,1:T(8,128)(2,1)}, u32[]{:S(2)}, u32[]{:S(2)}) async-start(bf16[32,256,128]{2,0,1:T(8,128)(2,1)} %copy.260), calls=%async_computation.7 | async-start | bytes 4194304 | tf_op jit(solution)/shard_map/all_to_all | solution.py:68
  361.0 192.1 %all-reduce.15.cloned.1.call-start = ((), (), s32[]{:S(2)}) async-start(), calls=%async_computation.12 | async-start | bytes 1572864 | tf_op jit(solution)/shard_map/psum | solution.py:173
  371.1 3.1 copy-start.11
  371.1 3.1 copy-start.13
  371.1 3.1 copy-start.14
  374.2 2.1 copy-start.6
  412.4 1.6 copy-start.8
  412.4 1.6 copy-start.9
  413.9 139.3 %copy-start.16 = (f32[32,16]{0,1:T(8,128)S(1)}, f32[32,16]{0,1:T(8,128)}, u32[]{:S(2)}) copy-start(f32[32,16]{0,1:T(8,128)} %copy-done.15) | copy-start | bytes 6148
  413.9 216.9 %all-reduce.17.cloned.1.call-start = ((), (), s32[]{:S(2)}) async-start(), calls=%async_computation.13 | async-start | bytes 1572864 | tf_op jit(solution)/shard_map/psum | solution.py:173
  (11 other events, 10.9 us)
Sparse Core Ops, SparseCore 0:
  14.2 58.0 all-gather.4
  100.5 45.2 all-gather.6
  157.6 47.5 all-gather.8
  304.3 48.0 all-gather.10
  414.0 139.0 all-reduce.14
  555.8 74.9 all-reduce.16
